TPU v7x, 32 devices: a whole 2x2x4 slice. The times are simulated.
32 devices in a mesh: row: 8 (over y, x, core), rep: 4 (over z).
Axes of the slice: x: 2, y: 2, z: 4, core: 2. Of those that a mesh axis runs over, the one named last changes fastest.
Arguments:
- features: bfloat16 [8192, 512], P(('row', 'rep')), may hold values from -6 to 6
- tiles: bfloat16 [64, 8, 128, 128], P(('row', 'rep')), may hold values from -0.1875 to 0.1875
- columns: int32 [64, 8], P(('row', 'rep')), may hold values from 0 to 63, as said below
- w_aggregate: bfloat16 [512, 512], replicated, may hold values from -0.25 to 0.25
- w_self: bfloat16 [512, 512], replicated, may hold values from -0.25 to 0.25
- w_middle: bfloat16 [512, 512], replicated, may hold values from -0.25 to 0.25
- w_output: bfloat16 [512, 512], replicated, may hold values from -0.25 to 0.25
- cotangent: bfloat16 [8192, 512], P(('row', 'rep')), may hold values from -6 to 6
Outputs:
- updated: bfloat16 [8192, 512], P(('row', 'rep'))
- grad_features: bfloat16 [8192, 512], P(('row', 'rep'))
- grad_output: float32 [512, 512], P('rep')
- grad_middle: float32 [512, 512], P('rep')
- grad_aggregate: float32 [512, 512], P('rep')
- grad_self: float32 [512, 512], P('rep')
Inputs may be any that keep to these rules, and one draw needn't show every extreme that they name: `columns`: row group g holds row blocks g * 8 to (g + 1) * 8 - 1, for g < 8. Every column block named by a row block of group g lies in group g - 1, g or g + 1, taken modulo 8; every row block names each of these three groups at least once. Column blocks may repeat within a row block.
All inputs are finite; a program needn't handle non-finite values.
Results may differ from a plain program's by a relative error of at most 0.015.
Values may be sent and summed in bfloat16 or wider, within the bound.
No kernel may reach another device: no remote copies, remote signals or barrier semaphores. Data moves between devices by JAX's collectives and lax.ppermute only.
A program may use at most 192 MiB of HBM per device.

v0:
```python
import math
import jax
import jax.numpy as jnp
from jax import lax
from jax.sharding import PartitionSpec as P


def from_behind(value, axis, steps):
    count = lax.axis_size(axis)
    pairs = [(source, (source + steps) % count) for source in range(count)]
    return lax.ppermute(value, axis, pairs)


def silu_slope(value):
    sig = jax.nn.sigmoid(value)
    return sig * (1.0 + value * (1.0 - sig))


def times_transposed(left_operand, weight):
    return lax.dot_general(
        left_operand, weight, (((1,), (1,)), ((), ())), preferred_element_type=jnp.float32
    )


def local(features, tiles, columns, w_aggregate, w_self, w_middle, w_output, cotangent):
    blocks_dev, width_k, tile_size, _ = tiles.shape
    width = features.shape[1]
    groups = lax.axis_size("row")
    replicas = lax.axis_size("rep")
    panel_blocks = replicas * blocks_dev
    panel_rows = panel_blocks * tile_size
    group_id = lax.axis_index("row")
    slot_of = (columns // panel_blocks - group_id + 1) % groups
    window_index = slot_of * panel_blocks + columns % panel_blocks
    own_panel = lax.all_gather(features, "rep", axis=0, tiled=True)
    prior_panel = from_behind(own_panel, "row", 1)
    next_panel = from_behind(own_panel, "row", -1)
    window = jnp.concatenate([prior_panel, own_panel, next_panel], 0).reshape(
        3 * panel_blocks, tile_size, width
    )
    picked = window[window_index]
    summed = jnp.einsum("bkij,bkjf->bif", tiles, picked, preferred_element_type=jnp.float32)
    aggregate = summed.reshape(blocks_dev * tile_size, width).astype(jnp.bfloat16)
    pre_first = jnp.dot(aggregate, w_aggregate, preferred_element_type=jnp.float32) + jnp.dot(
        features, w_self, preferred_element_type=jnp.float32
    )
    first = jax.nn.silu(pre_first).astype(jnp.bfloat16)
    pre_second = jnp.dot(first, w_middle, preferred_element_type=jnp.float32)
    second = jax.nn.silu(pre_second).astype(jnp.bfloat16)
    updated = (
        features.astype(jnp.float32) + jnp.dot(second, w_output, preferred_element_type=jnp.float32)
    ).astype(jnp.bfloat16)
    delta_second = (times_transposed(cotangent, w_output) * silu_slope(pre_second)).astype(
        jnp.bfloat16
    )
    delta_first = (times_transposed(delta_second, w_middle) * silu_slope(pre_first)).astype(
        jnp.bfloat16
    )
    delta_aggregate = times_transposed(delta_first, w_aggregate).astype(jnp.bfloat16)
    delta_blocks = delta_aggregate.reshape(blocks_dev, tile_size, width)
    messages = jnp.einsum("bkji,bjf->bkif", tiles, delta_blocks, preferred_element_type=jnp.float32)
    spread = jnp.zeros((3 * panel_blocks, tile_size, width), jnp.float32)
    spread = spread.at[window_index.reshape(-1)].add(messages.reshape(-1, tile_size, width))
    spread = spread.reshape(3 * panel_rows, width)
    prior_part = spread[:panel_rows]
    own_part = spread[panel_rows : 2 * panel_rows]
    next_part = spread[2 * panel_rows :]
    from_next = from_behind(prior_part.astype(jnp.bfloat16), "row", -1).astype(prior_part.dtype)
    from_prior = from_behind(next_part.astype(jnp.bfloat16), "row", 1).astype(next_part.dtype)
    returned = lax.psum_scatter(
        (own_part + from_next + from_prior).astype(jnp.bfloat16),
        "rep",
        scatter_dimension=0,
        tiled=True,
    ).astype(jnp.float32)
    grad_features = (
        cotangent.astype(jnp.float32) + times_transposed(delta_first, w_self) + returned
    ).astype(jnp.bfloat16)
    total_nodes = features.shape[0] * groups * replicas
    scale = 1.0 / math.sqrt(total_nodes)
    local_output = jnp.dot(second.T, cotangent, preferred_element_type=jnp.float32)
    local_middle = jnp.dot(first.T, delta_second, preferred_element_type=jnp.float32)
    local_aggregate = jnp.dot(aggregate.T, delta_first, preferred_element_type=jnp.float32)
    local_self = jnp.dot(features.T, delta_first, preferred_element_type=jnp.float32)
    shares = (
        lax.psum_scatter(
            local_output.astype(jnp.bfloat16), "rep", scatter_dimension=0, tiled=True
        ).astype(jnp.float32),
        lax.psum_scatter(
            local_middle.astype(jnp.bfloat16), "rep", scatter_dimension=0, tiled=True
        ).astype(jnp.float32),
        lax.psum_scatter(
            local_aggregate.astype(jnp.bfloat16), "rep", scatter_dimension=0, tiled=True
        ).astype(jnp.float32),
        lax.psum_scatter(
            local_self.astype(jnp.bfloat16), "rep", scatter_dimension=0, tiled=True
        ).astype(jnp.float32),
    )
    totals = (
        lax.psum(shares[0].astype(jnp.bfloat16), "row").astype(jnp.float32),
        lax.psum(shares[1].astype(jnp.bfloat16), "row").astype(jnp.float32),
        lax.psum(shares[2].astype(jnp.bfloat16), "row").astype(jnp.float32),
        lax.psum(shares[3].astype(jnp.bfloat16), "row").astype(jnp.float32),
    )
    return (
        updated,
        grad_features,
        totals[0] * scale,
        totals[1] * scale,
        totals[2] * scale,
        totals[3] * scale,
    )


def solution(mesh):
    placed = (
        P(("row", "rep"), None),
        P(("row", "rep"), None, None, None),
        P(("row", "rep"), None),
        P(),
        P(),
        P(),
        P(),
        P(("row", "rep"), None),
    )
    return jax.shard_map(
        local,
        mesh=mesh,
        in_specs=placed,
        out_specs=(
            P(("row", "rep"), None),
            P(("row", "rep"), None),
            P("rep", None),
            P("rep", None),
            P("rep", None),
            P("rep", None),
        ),
        check_vma=False,
    )
```

profile of v0, /device:TPU:0, one launch (start us, length us, event | category | flops | bytes accessed | tf_op | source)
XLA Modules:
  0.0 258.1 jit_solution(4128961649939991356)
XLA Ops:
  7.2 0.7 all-gather.2.cloned.1.call-update
  7.9 0.0 reduce-scatter.10.cloned.1.call-start
  8.0 32.3 %all-gather.2.cloned.1.call-done = bf16[1024,512]{1,0:T(8,128)(2,1)} async-done(((bf16[256,512]{1,0:T(8,128)(2,1)}), bf16[1024,512]{1,0:T(8,128)(2,1)}) %all-gather.2.cloned.1.call-update) | async-done | bytes 1048592 | tf_op jit(solution)/shard_map/all_gather | solution.py:35
  40.3 1.3 collective-permute-start.1
  41.6 0.7 compare_select_fusion
  42.3 0.1 reshape.66
  42.4 22.6 %collective-permute-done.1 = bf16[1024,512]{1,0:T(8,128)(2,1)S(1)} collective-permute-done((bf16[1024,512]{1,0:T(8,128)(2,1)}, bf16[1024,512]{1,0:T(8,128)(2,1)S(1)}, u32[]{:S(2)}, u32[]{:S(2)}) %collective-permute-start.1) | collective-permute-done | bytes 1048608 | tf_op jit(solution)/shard_map/ppermute | solution.py:11
  65.1 1.8 collective-permute-done
  66.9 2.8 %pad_maximum_fusion = bf16[3072,512]{1,0:T(8,128)(2,1)} fusion(bf16[1024,512]{1,0:T(8,128)(2,1)S(1)} %collective-permute-done.1, bf16[1024,512]{1,0:T(8,128)(2,1)} %all-gather.2.cloned.1.call-done, bf16[1024,512]{1,0:T(8,128)(2,1)S(1)} %collective-permute-done), kind=kLoop, calls=%fused_computation.2 | loop fusion | flops 9437184 | bytes 6291456 | tf_op jit(solution)/shard_map/concatenate | solution.py:38
  69.7 2.6 gather_fusion
  72.3 0.4 fusion.3
  72.8 0.5 copy-done.4
  73.3 0.3 fusion.14
  73.6 0.3 convolution_add_fusion.2
  73.9 0.3 fusion.11
  74.3 0.4 fusion.5
  74.7 0.7 copy-done.13
  75.4 1.2 convolution_convert_fusion.2
  76.6 0.0 reduce-scatter.12.cloned.1.call-start
  76.7 1.4 fusion.6
  78.1 1.1 convolution_convert_fusion.1
  79.2 0.0 reduce-scatter.8.cloned.1.call-start
  79.3 0.1 reshape.61
  79.4 1.2 convolution_convert_fusion.3
  80.6 0.0 reduce-scatter.14.cloned.1.call-start
  80.6 0.3 convolution_convert_fusion.4
  81.0 2.7 %fusion.15 = f32[2,512,8,128]{3,1,2,0:T(8,128)} fusion(bf16[2,128,512,1]{2,1,3,0:T(8,128)(2,1)S(1)} %bitcast.59, bf16[2,8,128,128]{3,2,1,0:T(8,128)(2,1)S(1)} %copy-done), kind=kOutput, calls=%fused_computation.49 | convolution fusion | flops 268435456 | bytes 4980736 | tf_op jit(solution)/shard_map/bkji,bjf->bkif/dot_general | solution.py:61
  83.6 5.4 %copy.15 = f32[16,128,512]{2,1,0:T(8,128)} copy(f32[16,128,512]{1,2,0:T(8,128)} %bitcast.54) | data formatting | bytes 8388608 | tf_op jit(solution)/shard_map/reshape | solution.py:63
  89.0 3.5 %broadcast_in_dim.8 = f32[24,128,512]{2,1,0:T(8,128)} broadcast(f32[]{:T(128)} %constant.53.clone.1), dimensions={} | broadcast | bytes 6291460 | tf_op jit(solution)/shard_map/broadcast_in_dim | solution.py:62
  92.5 9.6 %scatter_fusion = f32[24,128,512]{2,1,0:T(8,128)} fusion(f32[24,128,512]{2,1,0:T(8,128)} %broadcast_in_dim.8, s32[16]{0:T(128)S(1)} %fusion.10, f32[16,128,512]{2,1,0:T(8,128)} %copy.15), kind=kCustom, calls=%fused_computation.1 | custom fusion | flops 1048576 | bytes 12582976 | tf_op jit(solution)/shard_map/scatter-add | solution.py:63
  102.0 3.4 %convert.4 = bf16[24,128,512]{2,1,0:T(8,128)(2,1)S(1)} convert(f32[24,128,512]{2,1,0:T(8,128)} %scatter_fusion) | non-fusion elementwise | flops 1572864 | bytes 9437184 | tf_op jit(solution)/shard_map/convert.1
  105.4 1.6 fusion.13
  107.0 1.2 fusion.2
  108.2 0.0 all-reduce.3.cloned.1.call-start
  108.3 2.7 %collective-permute-start.2 = (bf16[1024,512]{1,0:T(8,128)(2,1)}, bf16[1024,512]{1,0:T(8,128)(2,1)}, u32[]{:S(2)}, u32[]{:S(2)}) collective-permute-start(bf16[1024,512]{1,0:T(8,128)(2,1)} %bitcast.12), channel_id=1, source_target_pairs={{0,28},{4,0},{8,4},{12,8},{16,12},{20,16},{24,20},{28,24},{1,29},{... | collective-permute-start | bytes 3145736 | tf_op jit(solution)/shard_map/ppermute | solution.py:11
  111.0 1.9 slice.22
  112.9 6.7 %reduce-scatter.12.cloned.1.call-done = bf16[128,512]{1,0:T(8,128)(2,1)} async-done(((bf16[512,512]{1,0:T(8,128)(2,1)}), bf16[128,512]{1,0:T(8,128)(2,1)}) %reduce-scatter.12.cloned.1.call-update) | async-done | bytes 131088 | tf_op jit(solution)/shard_map/reduce_scatter | solution.py:92
  119.5 22.2 %reduce-scatter.8.cloned.1.call-done = bf16[128,512]{1,0:T(8,128)(2,1)} async-done(((bf16[512,512]{1,0:T(8,128)(2,1)}), bf16[128,512]{1,0:T(8,128)(2,1)}) %reduce-scatter.8.cloned.1.call-update) | async-done | bytes 131088 | tf_op jit(solution)/shard_map/reduce_scatter | solution.py:86
  141.8 22.2 %reduce-scatter.14.cloned.1.call-done = bf16[128,512]{1,0:T(8,128)(2,1)} async-done(((bf16[512,512]{1,0:T(8,128)(2,1)}), bf16[128,512]{1,0:T(8,128)(2,1)}) %reduce-scatter.14.cloned.1.call-update) | async-done | bytes 131088 | tf_op jit(solution)/shard_map/reduce_scatter | solution.py:95
  164.0 0.0 reduce-scatter.6.cloned.1.call-start
  164.1 3.2 %fusion.1 = bf16[1024,512]{1,0:T(8,128)(2,1)} fusion(f32[8,128,512]{2,1,0:T(8,128)S(1)} %slice.22, bf16[1024,512]{1,0:T(8,128)(2,1)} %collective-permute-done.3, bf16[1024,512]{1,0:T(8,128)(2,1)} %collective-permute-done.2), kind=kLoop, calls=%fused_computation.5 | loop fusion | flops 2621440 | bytes 5242880 | tf_op jit(solution)/shard_map/convert_element_type | solution.py:71
  167.4 2.3 fusion.4
  169.7 0.3 convolution_add_fusion
  170.0 50.6 %all-reduce.3.cloned.1.call-done = (bf16[128,512]{1,0:T(8,128)(2,1)}, bf16[128,512]{1,0:T(8,128)(2,1)}, bf16[128,512]{1,0:T(8,128)(2,1)}, bf16[128,512]{1,0:T(8,128)(2,1)}) async-done(((bf16[128,512]{1,0:T(8,128)(2,1)}, bf16[128,512]{1,0:T(8,128)(2,1)}, bf16[128,512]{1,0:T(8,128)(2,1)}, bf16[128,512]{1,0:T(8,128)(2,1)}), (bf16[128,512]{1,0:T(8,128)(2,1)}, bf16[128,512]{1,0:T(8,128)(2,1)}, ...) | async-done | bytes 524304 | tf_op jit(solution)/shard_map/psum | solution.py:100
  220.6 1.8 convert_multiply_fusion.2
  222.4 1.8 convert_multiply_fusion
  224.2 25.3 %reduce-scatter.6.cloned.1.call-done = bf16[256,512]{1,0:T(8,128)(2,1)} async-done(((bf16[1024,512]{1,0:T(8,128)(2,1)}), bf16[256,512]{1,0:T(8,128)(2,1)}) %reduce-scatter.6.cloned.1.call-update) | async-done | bytes 262160 | tf_op jit(solution)/shard_map/reduce_scatter | solution.py:70
  249.6 1.7 add_convert_fusion
  (40 shorter events, 0.3 us)
Async XLA Ops:
  7.2 65.1 %copy-start = (bf16[2,8,128,128]{3,2,1,0:T(8,128)(2,1)S(1)}, bf16[2,8,128,128]{3,2,1,0:T(8,128)(2,1)}, u32[]{:S(2)}) copy-start(bf16[2,8,128,128]{3,2,1,0:T(8,128)(2,1)} %param.9) | copy-start | bytes 1572868
  7.2 33.1 %all-gather.2.cloned.1.call-start = ((), (), s32[]{:S(2)}) async-start(), calls=%async_computation.5 | async-start | bytes 1310720 | tf_op jit(solution)/shard_map/all_gather | solution.py:35
  7.9 104.9 %reduce-scatter.10.cloned.1.call-start = ((), (), s32[]{:S(2)}) async-start(), calls=%async_computation.8 | async-start | bytes 655360 | tf_op jit(solution)/shard_map/reduce_scatter | solution.py:89
  40.3 24.8 %collective-permute-start.1 = (bf16[1024,512]{1,0:T(8,128)(2,1)}, bf16[1024,512]{1,0:T(8,128)(2,1)S(1)}, u32[]{:S(2)}, u32[]{:S(2)}) collective-permute-start(bf16[1024,512]{1,0:T(8,128)(2,1)} %all-gather.2.cloned.1.call-done), channel_id=1, source_target_pairs={{0,28},{4,0},{8,4},{12,8},{16,12},{20,16},{24,20},{28,24},{1,29},{... | collective-permute-start | bytes 3145736 | tf_op jit(solution)/shard_map/ppermute | solution.py:11
  41.6 25.3 %collective-permute-start = (bf16[1024,512]{1,0:T(8,128)(2,1)}, bf16[1024,512]{1,0:T(8,128)(2,1)S(1)}, u32[]{:S(2)}, u32[]{:S(2)}) collective-permute-start(bf16[1024,512]{1,0:T(8,128)(2,1)} %all-gather.2.cloned.1.call-done), channel_id=1, source_target_pairs={{0,4},{4,8},{8,12},{12,16},{16,20},{20,24},{24,28},{28,0},{1,5},{5... | collective-permute-start | bytes 3145736 | tf_op jit(solution)/shard_map/ppermute | solution.py:11
  72.3 1.0 copy-start.4
  72.3 1.3 copy-start.1
  72.3 1.3 copy-start.2
  72.3 1.6 copy-start.8
  72.8 1.5 copy-start.6
  72.8 1.5 copy-start.10
  74.3 2.3 copy-start.11
  74.3 2.4 copy-start.9
  74.7 0.7 copy-start.13
  76.6 2.8 %copy-start.12 = (f32[256,512]{1,0:T(8,128)S(1)}, f32[256,512]{1,0:T(8,128)}, u32[]{:S(2)}) copy-start(f32[256,512]{1,0:T(8,128)} %copy-done.11) | copy-start | bytes 1572868
  76.6 43.0 %reduce-scatter.12.cloned.1.call-start = ((), (), s32[]{:S(2)}) async-start(), calls=%async_computation.9 | async-start | bytes 655360 | tf_op jit(solution)/shard_map/reduce_scatter | solution.py:92
  78.1 2.5 copy-start.5
  79.2 62.6 %reduce-scatter.8.cloned.1.call-start = ((), (), s32[]{:S(2)}) async-start(), calls=%async_computation.7 | async-start | bytes 655360 | tf_op jit(solution)/shard_map/reduce_scatter | solution.py:86
  80.6 83.5 %reduce-scatter.14.cloned.1.call-start = ((), (), s32[]{:S(2)}) async-start(), calls=%async_computation.10 | async-start | bytes 655360 | tf_op jit(solution)/shard_map/reduce_scatter | solution.py:95
  107.0 57.1 %collective-permute-start.3 = (bf16[1024,512]{1,0:T(8,128)(2,1)}, bf16[1024,512]{1,0:T(8,128)(2,1)}, u32[]{:S(2)}, u32[]{:S(2)}) collective-permute-start(bf16[1024,512]{1,0:T(8,128)(2,1)} %bitcast.13), channel_id=1, source_target_pairs={{0,4},{4,8},{8,12},{12,16},{16,20},{20,24},{24,28},{28,0},{1,5},{5... | collective-permute-start | bytes 3145736 | tf_op jit(solution)/shard_map/ppermute | solution.py:11
  108.2 112.4 %all-reduce.3.cloned.1.call-start = ((), (), s32[]{:S(2)}) async-start(), calls=%async_computation.11 | async-start | bytes 1048576 | tf_op jit(solution)/shard_map/psum | solution.py:100
  108.3 55.8 %collective-permute-start.2 = (bf16[1024,512]{1,0:T(8,128)(2,1)}, bf16[1024,512]{1,0:T(8,128)(2,1)}, u32[]{:S(2)}, u32[]{:S(2)}) collective-permute-start(bf16[1024,512]{1,0:T(8,128)(2,1)} %bitcast.12), channel_id=1, source_target_pairs={{0,28},{4,0},{8,4},{12,8},{16,12},{20,16},{24,20},{28,24},{1,29},{... | collective-permute-start | bytes 3145736 | tf_op jit(solution)/shard_map/ppermute | solution.py:11
  164.0 85.5 %reduce-scatter.6.cloned.1.call-start = ((), (), s32[]{:S(2)}) async-start(), calls=%async_computation.6 | async-start | bytes 1310720 | tf_op jit(solution)/shard_map/reduce_scatter | solution.py:70
  167.3 2.3 copy-start.3
  167.3 2.3 copy-start.7
Sparse Core Ops, SparseCore 0:
  9.6 30.6 all-gather.1
  76.7 20.3 reduce-scatter.9
  99.4 20.0 reduce-scatter.11
  121.7 20.0 reduce-scatter.7
  143.9 20.0 reduce-scatter.13
  167.2 53.3 all-reduce.2
  222.9 26.6 reduce-scatter.5
where the time goes:
time: 259 us; the launch traced here: 258 us
  waiting for transfers between devices  185 us (71%)
  other arithmetic  25 us (10%)
  local copies, waits for them, and re-layouts  16.3 us (6%)
  between operations  14.4 us (6%)
  matrix products  13.4 us (5%)
  starting transfers between devices  4.32 us (2%)
    psum x1, waiting for transfers between devices, local(): lax.psum(shares[0].astype(jnp.bfloat16), 'row').astype(jnp.float32)  50.6 us
    all_gather x1, waiting for transfers between devices, local(): own_panel = lax.all_gather(features, 'rep', axis=0, tiled=True)  32.3 us
    reduce_scatter x1, waiting for transfers between devices, local(): lax.psum_scatter((own_part + from_next + from_prior).astype(jnp.bfloat16)...  25.3 us
    ppermute x4, waiting for transfers between devices, from_behind(): return lax.ppermute(value, axis, pairs)  24.5 us
    reduce_scatter x1, waiting for transfers between devices, local(): lax.psum_scatter(local_output.astype(jnp.bfloat16), 'rep', scatter_dimens...  22.2 us
    reduce_scatter x1, waiting for transfers between devices, local(): lax.psum_scatter(local_self.astype(jnp.bfloat16), 'rep', scatter_dimensio...  22.2 us
    scatter-add x1, other arithmetic, local(): spread.at[window_index.reshape(-1)]  9.55 us
    reduce_scatter x1, waiting for transfers between devices, local(): lax.psum_scatter(local_aggregate.astype(jnp.bfloat16), 'rep', scatter_dim...  6.68 us
  transfers between devices with their start and end apart: 11, of which 8 were waited for; matrix products, arithmetic and copies ran while one was open for 17% of the time, Pallas kernels for 0%

commit v1 on v0

--- a/solution.py
+++ b/solution.py
@@ -23,6 +23,23 @@
 
 
 def local(features, tiles, columns, w_aggregate, w_self, w_middle, w_output, cotangent):
+
+    def orders_feed(inner_x):
+        n_parts = lax.axis_size("rep")
+        line_up = [inner_x]
+        for src_i in tuple(range(n_parts - 1)):
+            line_up.append(
+                lax.ppermute(
+                    line_up[-1], "rep", perm=[(c, (c + 1) % n_parts) for c in range(n_parts)]
+                )
+            )
+        passed = jnp.roll(
+            jnp.concatenate(line_up[::-1], axis=0),
+            (lax.axis_index("rep") + 1) * inner_x.shape[0],
+            axis=0,
+        )
+        return passed
+
     blocks_dev, width_k, tile_size, _ = tiles.shape
     width = features.shape[1]
     groups = lax.axis_size("row")
@@ -32,7 +49,7 @@
     group_id = lax.axis_index("row")
     slot_of = (columns // panel_blocks - group_id + 1) % groups
     window_index = slot_of * panel_blocks + columns % panel_blocks
-    own_panel = lax.all_gather(features, "rep", axis=0, tiled=True)
+    own_panel = orders_feed(features)
     prior_panel = from_behind(own_panel, "row", 1)
     next_panel = from_behind(own_panel, "row", -1)
     window = jnp.concatenate([prior_panel, own_panel, next_panel], 0).reshape(

time: 259 us -> 254 us (0.981)
  waiting for transfers between devices: 185 us -> 178 us
    all_gather x1 -> x0, waiting for transfers between devices: 32.3 us -> none  [local(): own_panel = lax.all_gather(features, 'rep', axis=0, tiled=True)]
    ppermute x0 -> x3, waiting for transfers between devices: none -> 26.2 us  [orders_feed(): lax.ppermute(line_up[-1], 'rep', perm=[(c, (c + 1) % n_parts) for c in ra...]
    ppermute x0 -> x3, starting transfers between devices: none -> 3.11 us  [orders_feed(): lax.ppermute(line_up[-1], 'rep', perm=[(c, (c + 1) % n_parts) for c in ra...]
  transfers between devices with their start and end apart: 11 -> 13, of which waited for: 8 -> 10; matrix products, arithmetic and copies ran while one was open for 17% -> 16% of each run, Pallas kernels for 0% -> 0%
where the time goes in v1:
time: 254 us; the launch traced here: 253 us
  waiting for transfers between devices  178 us (70%)
  other arithmetic  24.2 us (10%)
  local copies, waits for them, and re-layouts  17.7 us (7%)
  between operations  14.4 us (6%)
  matrix products  12.5 us (5%)
  starting transfers between devices  6.6 us (3%)
    psum x1, waiting for transfers between devices, local(): lax.psum(shares[0].astype(jnp.bfloat16), 'row').astype(jnp.float32)  50.5 us
    ppermute x3, waiting for transfers between devices, orders_feed(): lax.ppermute(line_up[-1], 'rep', perm=[(c, (c + 1) % n_parts) for c in ra...  26.2 us
    ppermute x4, waiting for transfers between devices, from_behind(): return lax.ppermute(value, axis, pairs)  25.5 us
    reduce_scatter x1, waiting for transfers between devices, local(): lax.psum_scatter((own_part + from_next + from_prior).astype(jnp.bfloat16)...  25.2 us
    reduce_scatter x1, waiting for transfers between devices, local(): lax.psum_scatter(local_output.astype(jnp.bfloat16), 'rep', scatter_dimens...  22.4 us
    reduce_scatter x1, waiting for transfers between devices, local(): lax.psum_scatter(local_self.astype(jnp.bfloat16), 'rep', scatter_dimensio...  22.2 us
    scatter-add x1, other arithmetic, local(): spread.at[window_index.reshape(-1)]  9.53 us
    reduce_scatter x1, waiting for transfers between devices, local(): lax.psum_scatter(local_aggregate.astype(jnp.bfloat16), 'rep', scatter_dim...  5.55 us
  transfers between devices with their start and end apart: 13, of which 10 were waited for; matrix products, arithmetic and copies ran while one was open for 16% of the time, Pallas kernels for 0%

profile of v1, /device:TPU:0, one launch (start us, length us, event | category | flops | bytes accessed | tf_op | source)
XLA Modules:
  0.0 253.2 jit_solution(3386737388654672953)
XLA Ops:
  7.2 3.1 %collective-permute-start = (bf16[256,512]{1,0:T(8,128)(2,1)}, bf16[256,512]{1,0:T(8,128)(2,1)S(1)}, u32[]{:S(2)}, u32[]{:S(2)}) collective-permute-start(bf16[256,512]{1,0:T(8,128)(2,1)} %param.8), channel_id=1, source_target_pairs={{0,1},{1,2},{2,3},{3,0},{4,5},{5,6},{6,7},{7,4},{8,9},{9,10},{10,1... | collective-permute-start | bytes 786440 | tf_op jit(solution)/shard_map/ppermute | solution.py:32
  10.3 8.5 %collective-permute-done = bf16[256,512]{1,0:T(8,128)(2,1)S(1)} collective-permute-done((bf16[256,512]{1,0:T(8,128)(2,1)}, bf16[256,512]{1,0:T(8,128)(2,1)S(1)}, u32[]{:S(2)}, u32[]{:S(2)}) %collective-permute-start) | collective-permute-done | bytes 262176 | tf_op jit(solution)/shard_map/ppermute | solution.py:32
  18.9 9.3 %collective-permute-done.1 = bf16[256,512]{1,0:T(8,128)(2,1)S(1)} collective-permute-done((bf16[256,512]{1,0:T(8,128)(2,1)S(1)}, bf16[256,512]{1,0:T(8,128)(2,1)S(1)}, u32[]{:S(2)}, u32[]{:S(2)}) %collective-permute-start.1) | collective-permute-done | bytes 262176 | tf_op jit(solution)/shard_map/ppermute | solution.py:32
  28.2 8.4 %collective-permute-done.2 = bf16[256,512]{1,0:T(8,128)(2,1)S(1)} collective-permute-done((bf16[256,512]{1,0:T(8,128)(2,1)S(1)}, bf16[256,512]{1,0:T(8,128)(2,1)S(1)}, u32[]{:S(2)}, u32[]{:S(2)}) %collective-permute-start.2) | collective-permute-done | bytes 262176 | tf_op jit(solution)/shard_map/ppermute | solution.py:32
  36.6 1.0 constant_dynamic-update-slice_fusion.4
  37.8 0.1 constant_dynamic-slice_fusion
  37.8 0.1 collective-permute-start.4
  37.9 0.5 collective-permute-start.3
  38.4 0.1 reshape.66
  38.5 22.4 %collective-permute-done.4 = bf16[1024,512]{1,0:T(8,128)(2,1)S(1)} collective-permute-done((bf16[1024,512]{1,0:T(8,128)(2,1)S(1)}, bf16[1024,512]{1,0:T(8,128)(2,1)S(1)}, u32[]{:S(2)}, u32[]{:S(2)}) %collective-permute-start.4) | collective-permute-done | bytes 1048608 | tf_op jit(solution)/shard_map/ppermute | solution.py:11
  60.9 3.1 %collective-permute-done.3 = bf16[1024,512]{1,0:T(8,128)(2,1)} collective-permute-done((bf16[1024,512]{1,0:T(8,128)(2,1)S(1)}, bf16[1024,512]{1,0:T(8,128)(2,1)}, u32[]{:S(2)}, u32[]{:S(2)}) %collective-permute-start.3) | collective-permute-done | bytes 1048608 | tf_op jit(solution)/shard_map/ppermute | solution.py:11
  64.0 2.8 %pad_maximum_fusion = bf16[3072,512]{1,0:T(8,128)(2,1)} fusion(bf16[1024,512]{1,0:T(8,128)(2,1)S(1)} %collective-permute-done.4, bf16[1024,512]{1,0:T(8,128)(2,1)S(1)} %constant_dynamic-slice_fusion, bf16[1024,512]{1,0:T(8,128)(2,1)} %collective-permute-done.3), kind=kLoop, calls=%fused_computation.2 | loop fusion | flops 9437184 | bytes 6291456 | tf_op jit(solution)/shard_map/concatenate | solution.py:55
  66.8 2.6 %gather_fusion = bf16[16,128,512]{2,1,0:T(8,128)(2,1)S(1)} fusion(bf16[24,128,512]{2,1,0:T(8,128)(2,1)} %bitcast.55, s32[1024]{0:T(1024)S(1)} %pad_clamp_fusion), kind=kCustom, calls=%fused_computation | custom fusion | bytes 4194368 | tf_op jit(solution)/shard_map/gather | solution.py:58
  69.4 0.4 fusion.3
  69.9 0.5 copy-done.4
  70.4 0.3 fusion.14
  70.8 0.3 convolution_add_fusion.2
  71.1 0.3 fusion.11
  71.4 0.3 copy-done.6
  71.7 0.2 copy-done.10
  71.9 0.4 fusion.5
  72.3 0.4 copy-done.11
  72.7 1.2 convolution_convert_fusion.2
  74.0 0.4 fusion.6
  74.3 1.1 convolution_convert_fusion.1
  75.5 0.1 reshape.61
  75.6 1.2 convolution_convert_fusion.3
  76.9 0.3 convolution_convert_fusion.4
  77.2 2.7 %fusion.15 = f32[2,512,8,128]{3,1,2,0:T(8,128)} fusion(bf16[2,128,512,1]{2,1,3,0:T(8,128)(2,1)S(1)} %bitcast.59, bf16[2,8,128,128]{3,2,1,0:T(8,128)(2,1)S(1)} %copy-done), kind=kOutput, calls=%fused_computation.58 | convolution fusion | flops 268435456 | bytes 4980736 | tf_op jit(solution)/shard_map/bkji,bjf->bkif/dot_general | solution.py:78
  79.9 5.4 %copy.15 = f32[16,128,512]{2,1,0:T(8,128)} copy(f32[16,128,512]{1,2,0:T(8,128)} %bitcast.54) | data formatting | bytes 8388608 | tf_op jit(solution)/shard_map/reshape | solution.py:80
  85.3 3.5 %broadcast_in_dim.8 = f32[24,128,512]{2,1,0:T(8,128)} broadcast(f32[]{:T(128)} %constant.80.clone.1), dimensions={} | broadcast | bytes 6291460 | tf_op jit(solution)/shard_map/broadcast_in_dim | solution.py:79
  88.7 9.5 %scatter_fusion = f32[24,128,512]{2,1,0:T(8,128)} fusion(f32[24,128,512]{2,1,0:T(8,128)} %broadcast_in_dim.8, s32[16]{0:T(128)S(1)} %fusion.10, f32[16,128,512]{2,1,0:T(8,128)} %copy.15), kind=kCustom, calls=%fused_computation.1 | custom fusion | flops 1048576 | bytes 12582976 | tf_op jit(solution)/shard_map/scatter-add | solution.py:80
  98.3 3.3 %convert.4 = bf16[24,128,512]{2,1,0:T(8,128)(2,1)S(1)} convert(f32[24,128,512]{2,1,0:T(8,128)} %scatter_fusion) | non-fusion elementwise | flops 1572864 | bytes 9437184 | tf_op jit(solution)/shard_map/convert.1
  101.6 1.6 fusion.13
  103.2 1.2 fusion.2
  104.4 2.7 %collective-permute-start.5 = (bf16[1024,512]{1,0:T(8,128)(2,1)}, bf16[1024,512]{1,0:T(8,128)(2,1)}, u32[]{:S(2)}, u32[]{:S(2)}) collective-permute-start(bf16[1024,512]{1,0:T(8,128)(2,1)} %bitcast.12), channel_id=1, source_target_pairs={{0,28},{4,0},{8,4},{12,8},{16,12},{20,16},{24,20},{28,24},{1,29},{... | collective-permute-start | bytes 3145736 | tf_op jit(solution)/shard_map/ppermute | solution.py:11
  107.1 1.9 slice.22
  109.0 5.5 %reduce-scatter.12.cloned.1.call-done = bf16[128,512]{1,0:T(8,128)(2,1)} async-done(((bf16[512,512]{1,0:T(8,128)(2,1)}), bf16[128,512]{1,0:T(8,128)(2,1)}) %reduce-scatter.12.cloned.1.call-update) | async-done | bytes 131088 | tf_op jit(solution)/shard_map/reduce_scatter | solution.py:109
  114.6 22.4 %reduce-scatter.8.cloned.1.call-done = bf16[128,512]{1,0:T(8,128)(2,1)} async-done(((bf16[512,512]{1,0:T(8,128)(2,1)}), bf16[128,512]{1,0:T(8,128)(2,1)}) %reduce-scatter.8.cloned.1.call-update) | async-done | bytes 131088 | tf_op jit(solution)/shard_map/reduce_scatter | solution.py:103
  137.0 22.2 %reduce-scatter.14.cloned.1.call-done = bf16[128,512]{1,0:T(8,128)(2,1)} async-done(((bf16[512,512]{1,0:T(8,128)(2,1)}), bf16[128,512]{1,0:T(8,128)(2,1)}) %reduce-scatter.14.cloned.1.call-update) | async-done | bytes 131088 | tf_op jit(solution)/shard_map/reduce_scatter | solution.py:112
  159.3 3.2 %fusion.1 = bf16[1024,512]{1,0:T(8,128)(2,1)} fusion(f32[8,128,512]{2,1,0:T(8,128)S(1)} %slice.22, bf16[1024,512]{1,0:T(8,128)(2,1)} %collective-permute-done.6, bf16[1024,512]{1,0:T(8,128)(2,1)} %collective-permute-done.5), kind=kLoop, calls=%fused_computation.5 | loop fusion | flops 2621440 | bytes 5242880 | tf_op jit(solution)/shard_map/convert_element_type | solution.py:88
  162.6 2.3 fusion.4
  164.9 0.3 convolution_add_fusion
  165.2 50.5 %all-reduce.3.cloned.1.call-done = (bf16[128,512]{1,0:T(8,128)(2,1)}, bf16[128,512]{1,0:T(8,128)(2,1)}, bf16[128,512]{1,0:T(8,128)(2,1)}, bf16[128,512]{1,0:T(8,128)(2,1)}) async-done(((bf16[128,512]{1,0:T(8,128)(2,1)}, bf16[128,512]{1,0:T(8,128)(2,1)}, bf16[128,512]{1,0:T(8,128)(2,1)}, bf16[128,512]{1,0:T(8,128)(2,1)}), (bf16[128,512]{1,0:T(8,128)(2,1)}, bf16[128,512]{1,0:T(8,128)(2,1)}, ...) | async-done | bytes 524304 | tf_op jit(solution)/shard_map/psum | solution.py:117
  215.8 1.8 convert_multiply_fusion.2
  217.6 1.8 convert_multiply_fusion
  219.4 25.2 %reduce-scatter.6.cloned.1.call-done = bf16[256,512]{1,0:T(8,128)(2,1)} async-done(((bf16[1024,512]{1,0:T(8,128)(2,1)}), bf16[256,512]{1,0:T(8,128)(2,1)}) %reduce-scatter.6.cloned.1.call-update) | async-done | bytes 262160 | tf_op jit(solution)/shard_map/reduce_scatter | solution.py:87
  244.6 1.7 add_convert_fusion
  (50 shorter events, 0.6 us)
Async XLA Ops:
  7.2 62.2 %copy-start = (bf16[2,8,128,128]{3,2,1,0:T(8,128)(2,1)S(1)}, bf16[2,8,128,128]{3,2,1,0:T(8,128)(2,1)}, u32[]{:S(2)}) copy-start(bf16[2,8,128,128]{3,2,1,0:T(8,128)(2,1)} %param.9) | copy-start | bytes 1572868
  7.2 30.5 %copy-start.1 = (bf16[256,512]{1,0:T(8,128)(2,1)S(1)}, bf16[256,512]{1,0:T(8,128)(2,1)}, u32[]{:S(2)}) copy-start(bf16[256,512]{1,0:T(8,128)(2,1)} %param.8) | copy-start | bytes 786436
  7.2 101.8 %reduce-scatter.10.cloned.1.call-start = ((), (), s32[]{:S(2)}) async-start(), calls=%async_computation.7 | async-start | bytes 655360 | tf_op jit(solution)/shard_map/reduce_scatter | solution.py:106
  7.2 11.6 %collective-permute-start = (bf16[256,512]{1,0:T(8,128)(2,1)}, bf16[256,512]{1,0:T(8,128)(2,1)S(1)}, u32[]{:S(2)}, u32[]{:S(2)}) collective-permute-start(bf16[256,512]{1,0:T(8,128)(2,1)} %param.8), channel_id=1, source_target_pairs={{0,1},{1,2},{2,3},{3,0},{4,5},{5,6},{6,7},{7,4},{8,9},{9,10},{10,1... | collective-permute-start | bytes 786440 | tf_op jit(solution)/shard_map/ppermute | solution.py:32
  18.9 9.3 %collective-permute-start.1 = (bf16[256,512]{1,0:T(8,128)(2,1)S(1)}, bf16[256,512]{1,0:T(8,128)(2,1)S(1)}, u32[]{:S(2)}, u32[]{:S(2)}) collective-permute-start(bf16[256,512]{1,0:T(8,128)(2,1)S(1)} %collective-permute-done), channel_id=1, source_target_pairs={{0,1},{1,2},{2,3},{3,0},{4,5},{5,6},{6,7},{7,4},{8,9},{9,10},{10,1... | collective-permute-start | bytes 786440 | tf_op jit(solution)/shard_map/ppermute | solution.py:32
  28.2 8.4 %collective-permute-start.2 = (bf16[256,512]{1,0:T(8,128)(2,1)S(1)}, bf16[256,512]{1,0:T(8,128)(2,1)S(1)}, u32[]{:S(2)}, u32[]{:S(2)}) collective-permute-start(bf16[256,512]{1,0:T(8,128)(2,1)S(1)} %collective-permute-done.1), channel_id=1, source_target_pairs={{0,1},{1,2},{2,3},{3,0},{4,5},{5,6},{6,7},{7,4},{8,9},{9,10},{10,1... | collective-permute-start | bytes 786440 | tf_op jit(solution)/shard_map/ppermute | solution.py:32
  37.6 0.8 copy-start.8
  37.8 23.1 %collective-permute-start.4 = (bf16[1024,512]{1,0:T(8,128)(2,1)S(1)}, bf16[1024,512]{1,0:T(8,128)(2,1)S(1)}, u32[]{:S(2)}, u32[]{:S(2)}) collective-permute-start(bf16[1024,512]{1,0:T(8,128)(2,1)S(1)} %constant_dynamic-slice_fusion), channel_id=1, source_target_pairs={{0,28},{4,0},{8,4},{12,8},{16,12},{20,16},{24,20},{28,24},{1,29},{... | collective-permute-start | bytes 3145736 | tf_op jit(solution)/shard_map/ppermute | solution.py:11
  37.9 26.1 %collective-permute-start.3 = (bf16[1024,512]{1,0:T(8,128)(2,1)S(1)}, bf16[1024,512]{1,0:T(8,128)(2,1)}, u32[]{:S(2)}, u32[]{:S(2)}) collective-permute-start(bf16[1024,512]{1,0:T(8,128)(2,1)S(1)} %constant_dynamic-slice_fusion), channel_id=1, source_target_pairs={{0,4},{4,8},{8,12},{12,16},{16,20},{20,24},{24,28},{28,0},{1,5},{5... | collective-permute-start | bytes 3145736 | tf_op jit(solution)/shard_map/ppermute | solution.py:11
  69.4 1.0 copy-start.4
  69.4 1.3 copy-start.2
  69.9 1.2 copy-start.9
  70.7 1.0 copy-start.6
  70.8 1.1 copy-start.10
  71.9 0.8 copy-start.11
  73.9 1.7 copy-start.12
  73.9 40.7 %reduce-scatter.12.cloned.1.call-start = ((), (), s32[]{:S(2)}) async-start(), calls=%async_computation.8 | async-start | bytes 655360 | tf_op jit(solution)/shard_map/reduce_scatter | solution.py:109
  75.5 1.4 copy-start.5
  75.5 61.5 %reduce-scatter.8.cloned.1.call-start = ((), (), s32[]{:S(2)}) async-start(), calls=%async_computation.6 | async-start | bytes 655360 | tf_op jit(solution)/shard_map/reduce_scatter | solution.py:103
  76.8 82.4 %reduce-scatter.14.cloned.1.call-start = ((), (), s32[]{:S(2)}) async-start(), calls=%async_computation.9 | async-start | bytes 655360 | tf_op jit(solution)/shard_map/reduce_scatter | solution.py:112
  103.2 56.2 %collective-permute-start.6 = (bf16[1024,512]{1,0:T(8,128)(2,1)}, bf16[1024,512]{1,0:T(8,128)(2,1)}, u32[]{:S(2)}, u32[]{:S(2)}) collective-permute-start(bf16[1024,512]{1,0:T(8,128)(2,1)} %bitcast.13), channel_id=1, source_target_pairs={{0,4},{4,8},{8,12},{12,16},{16,20},{20,24},{24,28},{28,0},{1,5},{5... | collective-permute-start | bytes 3145736 | tf_op jit(solution)/shard_map/ppermute | solution.py:11
  104.4 111.4 %all-reduce.3.cloned.1.call-start = ((), (), s32[]{:S(2)}) async-start(), calls=%async_computation.10 | async-start | bytes 1048576 | tf_op jit(solution)/shard_map/psum | solution.py:117
  104.4 54.9 %collective-permute-start.5 = (bf16[1024,512]{1,0:T(8,128)(2,1)}, bf16[1024,512]{1,0:T(8,128)(2,1)}, u32[]{:S(2)}, u32[]{:S(2)}) collective-permute-start(bf16[1024,512]{1,0:T(8,128)(2,1)} %bitcast.12), channel_id=1, source_target_pairs={{0,28},{4,0},{8,4},{12,8},{16,12},{20,16},{24,20},{28,24},{1,29},{... | collective-permute-start | bytes 3145736 | tf_op jit(solution)/shard_map/ppermute | solution.py:11
  159.3 85.3 %reduce-scatter.6.cloned.1.call-start = ((), (), s32[]{:S(2)}) async-start(), calls=%async_computation.5 | async-start | bytes 1310720 | tf_op jit(solution)/shard_map/reduce_scatter | solution.py:87
  162.6 2.3 copy-start.3
  162.6 2.3 copy-start.7
Sparse Core Ops, SparseCore 0:
  74.0 18.1 reduce-scatter.9
  94.5 20.0 reduce-scatter.11
  116.9 20.0 reduce-scatter.7
  139.1 20.0 reduce-scatter.13
  162.4 53.3 all-reduce.2
  217.9 26.6 reduce-scatter.5
